TPU v7x, 256 devices: a whole 4x4x8 slice. The times are simulated.
256 devices in a mesh: member: 8 (over z), cell: 32 (over x, y, core).
Axes of the slice: x: 4, y: 4, z: 8, core: 2. Of those that a mesh axis runs over, the one named last changes fastest.
Arguments:
- prior: float32 [64, 524288], P('member', 'cell')
- samples: float32 [64, 524288], P('member', 'cell')
- noise: float32 [2, 64, 524288], P(None, 'member', 'cell'), may hold values from -6 to 6
- obs_cells: int32 [2, 65536], P(None, 'cell'), may hold values from 0 to 524287, as said below
- obs_values: float32 [2, 65536], P(None, 'cell'), may hold values from -6 to 6
- seismic_mask: int32 [2, 4096], P(None, 'cell'), may hold values 0 or 1
Outputs:
- analysis: float32 [64, 524288], P('member', 'cell')
Inputs may be any that keep to these rules, and one draw needn't show every extreme that they name: obs_cells[s, o] lies in cells k * 16384 to (k + 1) * 16384 - 1 where k = o // 2048; cells may repeat.
All inputs are finite; a program needn't handle non-finite values. No bound on the sum of `seismic_mask` on one device may be relied on, other than what follows from the above.
Results may differ from a plain program's by a relative error of at most 0.0003.
Values sent between devices are 32-bit elements; how exact they have to be, the bound alone decides.
No kernel may reach another device: no remote copies, remote signals or barrier semaphores. Data moves between devices by JAX's collectives and lax.ppermute only.
A program may use at most 64 MiB of HBM per device.

v0:
```python
import math
import jax
import jax.numpy as jnp
from jax import lax
from jax.sharding import PartitionSpec as P

STEPS = 2


def advance(state, fresh, prior_slab, prior_part, precision_slab, target_slab, step, ncell):
    time_now = 0.6 - 0.1 * step
    alpha = 1.0 - 0.95 * time_now
    drift = -0.95 / alpha
    diffusion = 1.0 - 2.0 * drift * time_now
    cross_part = lax.dot_general(
        state,
        prior_slab,
        (((1,), (1,)), ((), ())),
        precision=lax.Precision.HIGHEST,
        preferred_element_type=jnp.float32,
    )
    cross, prior_sq = lax.psum((cross_part, prior_part), ("member", "cell"))
    dist = alpha * alpha * prior_sq[None, :] - 2.0 * alpha * cross
    weights = jax.nn.softmax(-dist / (2.0 * time_now * math.sqrt(ncell)), axis=1)
    mean = jnp.dot(
        weights, prior_slab, precision=lax.Precision.HIGHEST, preferred_element_type=jnp.float32
    )
    score = (alpha * mean - state) / time_now - (1.0 - time_now) * (
        precision_slab[None, :] * state - target_slab[None, :]
    )
    return state - 0.1 * (drift * state - diffusion * score) + math.sqrt(0.1 * diffusion) * fresh


def per_device(prior, samples, noise, obs_cells, obs_values, seismic_mask):
    cells = prior.shape[1]
    groups = lax.axis_size("member")
    width = cells // groups
    ncell = cells * lax.axis_size("cell")
    shard = lax.axis_index("cell")
    member_pos = lax.axis_index("member")
    local = obs_cells - shard * cells
    precision_field = jnp.zeros((cells,), jnp.float32)
    target_field = jnp.zeros((cells,), jnp.float32)
    for survey in range(obs_cells.shape[0]):
        where = local[survey]
        flags = seismic_mask[survey].astype(jnp.float32)
        weight = flags[where // 128]
        precision_field = precision_field.at[where].add(weight)
        target_field = target_field.at[where].add(weight * obs_values[survey])
    precision_slab = lax.dynamic_slice_in_dim(precision_field, member_pos * width, width)
    target_slab = lax.dynamic_slice_in_dim(target_field, member_pos * width, width)
    prior_slab = lax.all_to_all(prior, "member", split_axis=1, concat_axis=0, tiled=True)
    prior_part = jnp.sum(prior_slab * prior_slab, axis=1)
    state = samples
    for step in range(STEPS):
        slab, fresh = (
            lax.all_to_all(state, "member", split_axis=1, concat_axis=0, tiled=True),
            lax.all_to_all(noise[step], "member", split_axis=1, concat_axis=0, tiled=True),
        )
        slab = advance(
            slab, fresh, prior_slab, prior_part, precision_slab, target_slab, step, ncell
        )
        state = lax.all_to_all(slab, "member", split_axis=0, concat_axis=1, tiled=True)
    return state


def solution(mesh):
    in_specs = (
        P("member", "cell"),
        P("member", "cell"),
        P(None, "member", "cell"),
        P(None, "cell"),
        P(None, "cell"),
        P(None, "cell"),
    )
    out_specs = P("member", "cell")
    return jax.shard_map(
        per_device, mesh=mesh, in_specs=in_specs, out_specs=out_specs, check_vma=False
    )
```

profile of v0, /device:TPU:2, one launch (start us, length us, event | category | flops | bytes accessed | tf_op | source)
XLA Modules:
  0.0 346.3 jit_solution(6709701843080657037)
XLA Ops:
  0.0 8.6 %all-to-all-start.1 = ((f32[8,8,2048]{2,0,1:T(8,128)}), f32[8,8,2048]{2,0,1:T(8,128)S(1)}, u32[]{:S(2)}, u32[]{:S(2)}) async-start(f32[8,8,2048]{2,0,1:T(8,128)} %bitcast.90), calls=%async_computation.1 | async-start | bytes 1048576 | tf_op jit(solution)/shard_map/all_to_all | solution.py:52
  8.6 0.0 copy-start.1
  8.6 1.0 fusion.55
  9.7 16.4 %all-to-all-done.1 = f32[8,8,2048]{2,0,1:T(8,128)S(1)} async-done(((f32[8,8,2048]{2,0,1:T(8,128)}), f32[8,8,2048]{2,0,1:T(8,128)S(1)}, u32[]{:S(2)}, u32[]{:S(2)}) %all-to-all-start.1) | async-done | bytes 524320 | tf_op jit(solution)/shard_map/all_to_all | solution.py:52
  26.1 3.5 %all-to-all-start = ((f32[8,8,2048]{2,0,1:T(8,128)}), f32[8,8,2048]{2,0,1:T(8,128)S(1)}, u32[]{:S(2)}, u32[]{:S(2)}) async-start(f32[8,8,2048]{2,0,1:T(8,128)} %bitcast), calls=%async_computation | async-start | bytes 1048576 | tf_op jit(solution)/shard_map/all_to_all | solution.py:57
  29.6 0.1 compare_select_fusion
  29.7 0.7 copy-done.2
  30.4 17.0 %all-to-all-done = f32[8,8,2048]{2,0,1:T(8,128)S(1)} async-done(((f32[8,8,2048]{2,0,1:T(8,128)}), f32[8,8,2048]{2,0,1:T(8,128)S(1)}, u32[]{:S(2)}, u32[]{:S(2)}) %all-to-all-start) | async-done | bytes 524320 | tf_op jit(solution)/shard_map/all_to_all | solution.py:57
  47.5 3.6 %all-to-all-start.2 = ((f32[8,8,2048]{2,0,1:T(8,128)}), f32[8,8,2048]{2,0,1:T(8,128)S(1)}, u32[]{:S(2)}, u32[]{:S(2)}) async-start(f32[8,8,2048]{2,0,1:T(8,128)} %bitcast.17), calls=%async_computation.2 | async-start | bytes 1048576 | tf_op jit(solution)/shard_map/all_to_all | solution.py:58
  51.1 12.6 %gather_fusion = f32[2048]{0:T(1024)S(1)} fusion(f32[128]{0:T(128)S(1)} %get-tuple-element.16, s32[2048]{0:T(1024)S(1)} %broadcast_clamp_fusion.1), kind=kCustom, calls=%fused_computation | custom fusion | bytes 24576 | tf_op jit(solution)/shard_map/gather | solution.py:47
  63.8 11.3 %scatter_custom_fusion = f32[16384]{0:T(1024)S(1)} fusion(s32[2048]{0:T(1024)S(1)} %bitcast.97, f32[2048]{0:T(1024)S(1)} %gather_fusion, f32[]{:T(128)} %constant.33.clone.1), kind=kCustom, calls=%fused_computation.51 | custom fusion | flops 2048 | bytes 65540 | tf_op jit(solution)/shard_map/scatter-add | solution.py:48
  75.0 11.3 %scatter_custom_fusion.2 = f32[16384]{0:T(1024)S(1)} fusion(s32[2048]{0:T(1024)S(1)} %bitcast.98, f32[2048]{0:T(1024)S(1)} %mul.145, f32[]{:T(128)} %constant.33.clone.1), kind=kCustom, calls=%fused_computation.49 | custom fusion | flops 2048 | bytes 65540 | tf_op jit(solution)/shard_map/scatter-add | solution.py:49
  86.3 12.6 %gather_fusion.1 = f32[2048]{0:T(1024)S(1)} fusion(f32[128]{0:T(128)S(1)} %get-tuple-element.15, s32[2048]{0:T(1024)S(1)} %broadcast_clamp_fusion), kind=kCustom, calls=%fused_computation.1 | custom fusion | bytes 24576 | tf_op jit(solution)/shard_map/gather | solution.py:47
  99.0 11.6 %scatter_fusion = f32[16384]{0:T(1024)S(1)} fusion(f32[16384]{0:T(1024)S(1)} %scatter_custom_fusion, s32[2048]{0:T(1024)S(1)} %bitcast.91, f32[2048]{0:T(1024)S(1)} %gather_fusion.1), kind=kCustom, calls=%fused_computation.3 | custom fusion | flops 2048 | bytes 32768 | tf_op jit(solution)/shard_map/scatter-add | solution.py:48
  110.5 11.6 %scatter_fusion.1 = f32[16384]{0:T(1024)S(1)} fusion(f32[16384]{0:T(1024)S(1)} %scatter_custom_fusion.2, s32[2048]{0:T(1024)S(1)} %bitcast.92, f32[2048]{0:T(1024)S(1)} %mul.146), kind=kCustom, calls=%fused_computation.5 | custom fusion | flops 2048 | bytes 32768 | tf_op jit(solution)/shard_map/scatter-add | solution.py:49
  122.1 0.1 fusion.27
  122.3 0.1 reduce_sum.30
  122.4 0.6 fusion.22
  122.9 76.2 %all-reduce = (f32[64,64]{1,0:T(8,128)S(1)}, f32[64]{0:T(128)S(1)}) all-reduce(f32[64,64]{1,0:T(8,128)S(1)} %fusion.22, f32[64]{0:T(128)S(1)} %reduce_sum.30), channel_id=1, replica_groups=mesh['member'=8,'cell'=32] {'member','cell'}, use_global_device_ids=true, to_apply=%region_2.3 | all-reduce | flops 4160 | bytes 33280 | tf_op jit(solution)/shard_map/psum | solution.py:22
  199.2 0.1 fusion.39
  199.3 0.2 fusion.37
  199.5 0.9 fusion.17
  200.3 23.0 %all_to_all.115 = f32[8,8,2048]{2,1,0:T(8,128)S(1)} all-to-all(f32[8,8,2048]{2,1,0:T(8,128)S(1)} %fusion.17), channel_id=1, replica_groups=mesh['member'=8,'cell'=32] {'member'}, dimensions={0} | all-to-all | bytes 1048576 | tf_op jit(solution)/shard_map/all_to_all | solution.py:63
  223.3 18.4 %all_to_all.116 = f32[8,8,2048]{2,0,1:T(8,128)S(1)} all-to-all(f32[8,8,2048]{2,0,1:T(8,128)S(1)} %bitcast.88), channel_id=1, replica_groups=mesh['member'=8,'cell'=32] {'member'}, dimensions={1} | all-to-all | bytes 1048576 | tf_op jit(solution)/shard_map/all_to_all | solution.py:57
  241.8 3.5 %all-to-all-start.5 = ((f32[8,8,2048]{2,0,1:T(8,128)}), f32[8,8,2048]{2,0,1:T(8,128)S(1)}, u32[]{:S(2)}, u32[]{:S(2)}) async-start(f32[8,8,2048]{2,0,1:T(8,128)} %bitcast.26), calls=%async_computation.5 | async-start | bytes 1048576 | tf_op jit(solution)/shard_map/all_to_all | solution.py:58
  245.3 0.6 fusion.19
  245.8 75.5 %psum.26 = f32[64,64]{1,0:T(8,128)S(1)} all-reduce(f32[64,64]{1,0:T(8,128)S(1)} %fusion.19), channel_id=1, replica_groups=mesh['member'=8,'cell'=32] {'member','cell'}, use_global_device_ids=true, to_apply=%region_9.10 | all-reduce | flops 4096 | bytes 32768 | tf_op jit(solution)/shard_map/psum | solution.py:22
  321.3 0.1 fusion.40
  321.4 0.2 fusion.38
  321.6 0.9 fusion.15
  322.5 23.0 %all_to_all.117 = f32[8,8,2048]{2,1,0:T(8,128)S(1)} all-to-all(f32[8,8,2048]{2,1,0:T(8,128)S(1)} %fusion.15), channel_id=1, replica_groups=mesh['member'=8,'cell'=32] {'member'}, dimensions={0} | all-to-all | bytes 1048576 | tf_op jit(solution)/shard_map/all_to_all | solution.py:63
  345.5 0.8 copy.10
  (18 shorter events, 0.1 us)
Async XLA Ops:
  0.0 8.6 %copy-start = (f32[2,8,16384]{2,1,0:T(8,128)S(1)}, f32[2,8,16384]{2,1,0:T(8,128)}, u32[]{:S(2)}) copy-start(f32[2,8,16384]{2,1,0:T(8,128)} %param.8) | copy-start | bytes 3145732
  0.0 26.1 %all-to-all-start.1 = ((f32[8,8,2048]{2,0,1:T(8,128)}), f32[8,8,2048]{2,0,1:T(8,128)S(1)}, u32[]{:S(2)}, u32[]{:S(2)}) async-start(f32[8,8,2048]{2,0,1:T(8,128)} %bitcast.90), calls=%async_computation.1 | async-start | bytes 1048576 | tf_op jit(solution)/shard_map/all_to_all | solution.py:52
  8.6 1.0 copy-start.1
  26.1 21.4 %all-to-all-start = ((f32[8,8,2048]{2,0,1:T(8,128)}), f32[8,8,2048]{2,0,1:T(8,128)S(1)}, u32[]{:S(2)}, u32[]{:S(2)}) async-start(f32[8,8,2048]{2,0,1:T(8,128)} %bitcast), calls=%async_computation | async-start | bytes 1048576 | tf_op jit(solution)/shard_map/all_to_all | solution.py:57
  29.7 0.7 copy-start.2
  47.5 3.6 %copy-start.3 = (s32[2,128]{1,0:T(2,128)S(1)}, s32[2,128]{1,0:T(2,128)}, u32[]{:S(2)}) copy-start(s32[2,128]{1,0:T(2,128)} %param.11) | copy-start | bytes 3076
  47.5 152.0 %all-to-all-start.2 = ((f32[8,8,2048]{2,0,1:T(8,128)}), f32[8,8,2048]{2,0,1:T(8,128)S(1)}, u32[]{:S(2)}, u32[]{:S(2)}) async-start(f32[8,8,2048]{2,0,1:T(8,128)} %bitcast.17), calls=%async_computation.2 | async-start | bytes 1048576 | tf_op jit(solution)/shard_map/all_to_all | solution.py:58
  241.8 79.9 %all-to-all-start.5 = ((f32[8,8,2048]{2,0,1:T(8,128)}), f32[8,8,2048]{2,0,1:T(8,128)S(1)}, u32[]{:S(2)}, u32[]{:S(2)}) async-start(f32[8,8,2048]{2,0,1:T(8,128)} %bitcast.26), calls=%async_computation.5 | async-start | bytes 1048576 | tf_op jit(solution)/shard_map/all_to_all | solution.py:58
where the time goes:
time: 347 us; the launch traced here: 346 us
  blocking collectives  216 us (62%)
  other arithmetic  46.5 us (13%)
  waiting for transfers between devices  33.5 us (10%)
  local copies, waits for them, and re-layouts  27.9 us (8%)
  starting transfers between devices  19.2 us (6%)
    psum x2, blocking collectives, advance(): cross, prior_sq = lax.psum((cross_part, prior_part), ('member', 'cell'))  152 us
    all_to_all x2, blocking collectives, per_device(): lax.all_to_all(slab, 'member', split_axis=0, concat_axis=1, tiled=True)  46 us
    gather x2, local copies, waits for them, and re-layouts, per_device(): weight = flags[where // 128]  25.2 us
    scatter-add x2, other arithmetic, per_device(): target_field = target_field.at[where].add(weight * obs_values[survey])  22.8 us
    scatter-add x2, other arithmetic, per_device(): precision_field = precision_field.at[where].add(weight)  22.8 us
    all_to_all x1, blocking collectives, per_device(): lax.all_to_all(state, 'member', split_axis=1, concat_axis=0, tiled=True)  18.4 us
    all_to_all x1, waiting for transfers between devices, per_device(): lax.all_to_all(state, 'member', split_axis=1, concat_axis=0, tiled=True)  17 us
    all_to_all x1, waiting for transfers between devices, per_device(): lax.all_to_all(prior, 'member', split_axis=1, concat_axis=0, tiled=True)  16.4 us
  transfers between devices with their start and end apart: 4, of which 2 were waited for; matrix products, arithmetic and copies ran while one was open for 21% of the time, Pallas kernels for 0%

commit v1 on v0

--- a/solution.py
+++ b/solution.py
@@ -5,6 +5,22 @@
 from jax.sharding import PartitionSpec as P
 
 STEPS = 2
+
+
+def pairwise_exchange(array, axis, split, join):
+    ways, here = (lax.axis_size(axis), lax.axis_index(axis))
+    width = array.shape[split] // ways
+    shape = list(array.shape)
+    shape[split] = width
+    height = shape[join]
+    shape[join] = height * ways
+    full = jnp.zeros(shape, array.dtype)
+    for mask in range(ways):
+        part = lax.dynamic_slice_in_dim(array, (here ^ mask) * width, width, axis=split)
+        if mask:
+            part = lax.ppermute(part, axis, [(d, d ^ mask) for d in range(ways)])
+        full = lax.dynamic_update_slice_in_dim(full, part, (here ^ mask) * height, axis=join)
+    return full
 
 
 def advance(state, fresh, prior_slab, prior_part, precision_slab, target_slab, step, ncell):
@@ -54,7 +70,7 @@
     state = samples
     for step in range(STEPS):
         slab, fresh = (
-            lax.all_to_all(state, "member", split_axis=1, concat_axis=0, tiled=True),
+            pairwise_exchange(state, "member", 1, 0),
             lax.all_to_all(noise[step], "member", split_axis=1, concat_axis=0, tiled=True),
         )
         slab = advance(

time: 347 us -> 339 us (0.977)
  starting transfers between devices: 19.2 us -> 48.2 us
  blocking collectives: 216 us -> 196 us
  waiting for transfers between devices: 33.5 us -> 15.1 us
    ppermute x0 -> x14, starting transfers between devices: none -> 32.1 us  [pairwise_exchange(): part = lax.ppermute(part, axis, [(d, d ^ mask) for d in range(ways)])]
    all_to_all x1 -> x0, blocking collectives: 18.4 us -> none  [per_device(): lax.all_to_all(state, 'member', split_axis=1, concat_axis=0, tiled=True)]
    all_to_all x1 -> x0, waiting for transfers between devices: 17 us -> none  [per_device(): lax.all_to_all(state, 'member', split_axis=1, concat_axis=0, tiled=True)]
    all_to_all x1, waiting for transfers between devices: 16.4 us -> 0.01 us  [per_device(): lax.all_to_all(prior, 'member', split_axis=1, concat_axis=0, tiled=True)]
    ppermute x0 -> x14, waiting for transfers between devices: none -> 15.1 us  [pairwise_exchange(): part = lax.ppermute(part, axis, [(d, d ^ mask) for d in range(ways)])]
    all_to_all x1 -> x0, starting transfers between devices: 3.5 us -> none  [per_device(): lax.all_to_all(state, 'member', split_axis=1, concat_axis=0, tiled=True)]
  transfers between devices with their start and end apart: 4 -> 17, of which waited for: 2 -> 5; matrix products, arithmetic and copies ran while one was open for 21% -> 22% of each run, Pallas kernels for 0% -> 0%
where the time goes in v1:
time: 339 us; the launch traced here: 338 us
  blocking collectives  196 us (58%)
  starting transfers between devices  48.2 us (14%)
  other arithmetic  46.5 us (14%)
  local copies, waits for them, and re-layouts  29.8 us (9%)
  waiting for transfers between devices  15.1 us (4%)
    psum x2, blocking collectives, advance(): cross, prior_sq = lax.psum((cross_part, prior_part), ('member', 'cell'))  151 us
    all_to_all x2, blocking collectives, per_device(): lax.all_to_all(slab, 'member', split_axis=0, concat_axis=1, tiled=True)  44.6 us
    ppermute x14, starting transfers between devices, pairwise_exchange(): part = lax.ppermute(part, axis, [(d, d ^ mask) for d in range(ways)])  32.1 us
    gather x2, local copies, waits for them, and re-layouts, per_device(): weight = flags[where // 128]  25.2 us
    scatter-add x2, other arithmetic, per_device(): precision_field = precision_field.at[where].add(weight)  22.8 us
    scatter-add x2, other arithmetic, per_device(): target_field = target_field.at[where].add(weight * obs_values[survey])  22.8 us
    ppermute x14, waiting for transfers between devices, pairwise_exchange(): part = lax.ppermute(part, axis, [(d, d ^ mask) for d in range(ways)])  15.1 us
    all_to_all x2, starting transfers between devices, per_device(): lax.all_to_all(noise[step], 'member', split_axis=1, concat_axis=0, tiled=...  9.84 us
  transfers between devices with their start and end apart: 17, of which 5 were waited for; matrix products, arithmetic and copies ran while one was open for 22% of the time, Pallas kernels for 0%

profile of v1, /device:TPU:2, one launch (start us, length us, event | category | flops | bytes accessed | tf_op | source)
XLA Modules:
  0.0 338.5 jit_solution(87303157790968444)
XLA Ops:
  0.0 1.0 copy-done.1
  1.1 2.0 collective-permute-start
  3.1 3.3 collective-permute-start.1
  6.4 6.4 %collective-permute-start.3 = (f32[8,2048]{1,0:T(8,128)S(1)}, f32[8,2048]{1,0:T(8,128)S(1)}, u32[]{:S(2)}, u32[]{:S(2)}) collective-permute-start(f32[8,2048]{1,0:T(8,128)S(1)} %get-tuple-element.19), channel_id=1, source_target_pairs={{0,128},{32,160},{64,192},{96,224},{128,0},{160,32},{192,64},{224,... | collective-permute-start | bytes 196616 | tf_op jit(solution)/shard_map/ppermute | solution.py:21
  12.8 6.3 %all-to-all-start = ((f32[8,8,2048]{2,0,1:T(8,128)}), f32[8,8,2048]{2,0,1:T(8,128)S(1)}, u32[]{:S(2)}, u32[]{:S(2)}) async-start(f32[8,8,2048]{2,0,1:T(8,128)} %bitcast), calls=%async_computation | async-start | bytes 1048576 | tf_op jit(solution)/shard_map/all_to_all | solution.py:68
  19.1 1.0 fusion.45
  20.3 0.7 copy-done.3
  21.7 12.6 %gather_fusion = f32[2048]{0:T(1024)S(1)} fusion(f32[128]{0:T(128)S(1)} %get-tuple-element.32, s32[2048]{0:T(1024)S(1)} %broadcast_clamp_fusion.1), kind=kCustom, calls=%fused_computation | custom fusion | bytes 24576 | tf_op jit(solution)/shard_map/gather | solution.py:63
  34.3 12.6 %gather_fusion.1 = f32[2048]{0:T(1024)S(1)} fusion(f32[128]{0:T(128)S(1)} %get-tuple-element.31, s32[2048]{0:T(1024)S(1)} %broadcast_clamp_fusion), kind=kCustom, calls=%fused_computation.1 | custom fusion | bytes 24576 | tf_op jit(solution)/shard_map/gather | solution.py:63
  46.9 11.3 %scatter_custom_fusion.2 = f32[16384]{0:T(1024)S(1)} fusion(s32[2048]{0:T(1024)S(1)} %bitcast.75, f32[2048]{0:T(1024)S(1)} %mul.222, f32[]{:T(128)} %constant.39.clone.1), kind=kCustom, calls=%fused_computation.35 | custom fusion | flops 2048 | bytes 65540 | tf_op jit(solution)/shard_map/scatter-add | solution.py:65
  58.2 11.6 %scatter_fusion.1 = f32[16384]{0:T(1024)S(1)} fusion(f32[16384]{0:T(1024)S(1)} %scatter_custom_fusion.2, s32[2048]{0:T(1024)S(1)} %bitcast.69, f32[2048]{0:T(1024)S(1)} %mul.223), kind=kCustom, calls=%fused_computation.5 | custom fusion | flops 2048 | bytes 32768 | tf_op jit(solution)/shard_map/scatter-add | solution.py:65
  69.8 11.3 %scatter_custom_fusion = f32[16384]{0:T(1024)S(1)} fusion(s32[2048]{0:T(1024)S(1)} %bitcast.76, f32[2048]{0:T(1024)S(1)} %gather_fusion, f32[]{:T(128)} %constant.39.clone.1), kind=kCustom, calls=%fused_computation.37 | custom fusion | flops 2048 | bytes 65540 | tf_op jit(solution)/shard_map/scatter-add | solution.py:64
  81.1 11.6 %scatter_fusion = f32[16384]{0:T(1024)S(1)} fusion(f32[16384]{0:T(1024)S(1)} %scatter_custom_fusion, s32[2048]{0:T(1024)S(1)} %bitcast.70, f32[2048]{0:T(1024)S(1)} %gather_fusion.1), kind=kCustom, calls=%fused_computation.3 | custom fusion | flops 2048 | bytes 32768 | tf_op jit(solution)/shard_map/scatter-add | solution.py:64
  92.7 4.2 %collective-permute-start.5 = (f32[8,2048]{1,0:T(8,128)S(1)}, f32[8,2048]{1,0:T(8,128)S(1)}, u32[]{:S(2)}, u32[]{:S(2)}) collective-permute-start(f32[8,2048]{1,0:T(8,128)S(1)} %get-tuple-element.24), channel_id=1, source_target_pairs={{0,192},{32,224},{64,128},{96,160},{128,64},{160,96},{192,0},{224,... | collective-permute-start | bytes 196616 | tf_op jit(solution)/shard_map/ppermute | solution.py:21
  97.7 2.4 collective-permute-done.5
  100.2 6.4 %all-to-all-start.1 = ((f32[8,8,2048]{2,0,1:T(8,128)}), f32[8,8,2048]{2,0,1:T(8,128)S(1)}, u32[]{:S(2)}, u32[]{:S(2)}) async-start(f32[8,8,2048]{2,0,1:T(8,128)} %bitcast.13), calls=%async_computation.1 | async-start | bytes 1048576 | tf_op jit(solution)/shard_map/all_to_all | solution.py:74
  107.3 76.6 %all-reduce = (f32[64,64]{1,0:T(8,128)S(1)}, f32[64]{0:T(128)S(1)}) all-reduce(f32[64,64]{1,0:T(8,128)S(1)} %fusion.14, f32[64]{0:T(128)S(1)} %reduce_sum.30), channel_id=1, replica_groups=mesh['member'=8,'cell'=32] {'member','cell'}, use_global_device_ids=true, to_apply=%region_2.3 | all-reduce | flops 4160 | bytes 33280 | tf_op jit(solution)/shard_map/psum | solution.py:38
  184.2 0.9 fusion.9
  185.1 23.0 %all_to_all.83 = f32[8,8,2048]{2,1,0:T(8,128)S(1)} all-to-all(f32[8,8,2048]{2,1,0:T(8,128)S(1)} %fusion.9), channel_id=1, replica_groups=mesh['member'=8,'cell'=32] {'member'}, dimensions={0} | all-to-all | bytes 1048576 | tf_op jit(solution)/shard_map/all_to_all | solution.py:79
  208.9 3.5 %all-to-all-start.3 = ((f32[8,8,2048]{2,0,1:T(8,128)}), f32[8,8,2048]{2,0,1:T(8,128)S(1)}, u32[]{:S(2)}, u32[]{:S(2)}) async-start(f32[8,8,2048]{2,0,1:T(8,128)} %bitcast.21), calls=%async_computation.3 | async-start | bytes 1048576 | tf_op jit(solution)/shard_map/all_to_all | solution.py:74
  212.4 2.8 collective-permute-start.8
  215.2 1.5 collective-permute-start.9
  216.7 4.5 %collective-permute-start.10 = (f32[8,2048]{1,0:T(8,128)S(1)}, f32[8,2048]{1,0:T(8,128)S(1)}, u32[]{:S(2)}, u32[]{:S(2)}) collective-permute-start(f32[8,2048]{1,0:T(8,128)S(1)} %get-tuple-element.12), channel_id=1, source_target_pairs={{0,128},{32,160},{64,192},{96,224},{128,0},{160,32},{192,64},{224,... | collective-permute-start | bytes 196616 | tf_op jit(solution)/shard_map/ppermute | solution.py:21
  221.2 4.1 %collective-permute-start.12 = (f32[8,2048]{1,0:T(8,128)S(1)}, f32[8,2048]{1,0:T(8,128)S(1)}, u32[]{:S(2)}, u32[]{:S(2)}) collective-permute-start(f32[8,2048]{1,0:T(8,128)S(1)} %get-tuple-element.10), channel_id=1, source_target_pairs={{0,192},{32,224},{64,128},{96,160},{128,64},{160,96},{192,0},{224,... | collective-permute-start | bytes 196616 | tf_op jit(solution)/shard_map/ppermute | solution.py:21
  225.3 9.2 %collective-permute-done.8 = f32[8,2048]{1,0:T(8,128)S(1)} collective-permute-done((f32[8,2048]{1,0:T(8,128)S(1)}, f32[8,2048]{1,0:T(8,128)S(1)}, u32[]{:S(2)}, u32[]{:S(2)}) %collective-permute-start.8) | collective-permute-done | bytes 65568 | tf_op jit(solution)/shard_map/ppermute | solution.py:21
  234.6 2.0 collective-permute-start.13
  236.9 1.2 collective-permute-done.11
  238.1 1.9 collective-permute-done.13
  240.6 74.3 %psum.26 = f32[64,64]{1,0:T(8,128)S(1)} all-reduce(f32[64,64]{1,0:T(8,128)S(1)} %fusion.11), channel_id=1, replica_groups=mesh['member'=8,'cell'=32] {'member','cell'}, use_global_device_ids=true, to_apply=%region_9.10 | all-reduce | flops 4096 | bytes 32768 | tf_op jit(solution)/shard_map/psum | solution.py:38
  315.3 0.8 fusion.8
  316.1 21.6 %all_to_all.84 = f32[8,8,2048]{2,1,0:T(8,128)S(1)} all-to-all(f32[8,8,2048]{2,1,0:T(8,128)S(1)} %fusion.8), channel_id=1, replica_groups=mesh['member'=8,'cell'=32] {'member'}, dimensions={0} | all-to-all | bytes 1048576 | tf_op jit(solution)/shard_map/all_to_all | solution.py:79
  337.7 0.8 copy.28
  (63 shorter events, 4.7 us)
Async XLA Ops:
  0.0 1.0 copy-start.1
  1.0 18.0 %copy-start = (f32[2,8,16384]{2,1,0:T(8,128)S(1)}, f32[2,8,16384]{2,1,0:T(8,128)}, u32[]{:S(2)}) copy-start(f32[2,8,16384]{2,1,0:T(8,128)} %param.8) | copy-start | bytes 3145732
  1.1 91.6 %collective-permute-start = (f32[8,2048]{1,0:T(8,128)S(1)}, f32[8,2048]{1,0:T(8,128)S(1)}, u32[]{:S(2)}, u32[]{:S(2)}) collective-permute-start(f32[8,2048]{1,0:T(8,128)S(1)} %get-tuple-element.22), channel_id=1, source_target_pairs={{0,32},{32,0},{64,96},{96,64},{128,160},{160,128},{192,224},{224,1... | collective-permute-start | bytes 196616 | tf_op jit(solution)/shard_map/ppermute | solution.py:21
  3.1 93.8 %collective-permute-start.1 = (f32[8,2048]{1,0:T(8,128)S(1)}, f32[8,2048]{1,0:T(8,128)S(1)}, u32[]{:S(2)}, u32[]{:S(2)}) collective-permute-start(f32[8,2048]{1,0:T(8,128)S(1)} %get-tuple-element.21), channel_id=1, source_target_pairs={{0,64},{32,96},{64,0},{96,32},{128,192},{160,224},{192,128},{224,1... | collective-permute-start | bytes 196616 | tf_op jit(solution)/shard_map/ppermute | solution.py:21
  6.4 91.2 %collective-permute-start.2 = (f32[8,2048]{1,0:T(8,128)S(1)}, f32[8,2048]{1,0:T(8,128)S(1)}, u32[]{:S(2)}, u32[]{:S(2)}) collective-permute-start(f32[8,2048]{1,0:T(8,128)S(1)} %get-tuple-element.20), channel_id=1, source_target_pairs={{0,96},{32,64},{64,32},{96,0},{128,224},{160,192},{192,160},{224,1... | collective-permute-start | bytes 196616 | tf_op jit(solution)/shard_map/ppermute | solution.py:21
  6.4 91.3 %collective-permute-start.3 = (f32[8,2048]{1,0:T(8,128)S(1)}, f32[8,2048]{1,0:T(8,128)S(1)}, u32[]{:S(2)}, u32[]{:S(2)}) collective-permute-start(f32[8,2048]{1,0:T(8,128)S(1)} %get-tuple-element.19), channel_id=1, source_target_pairs={{0,128},{32,160},{64,192},{96,224},{128,0},{160,32},{192,64},{224,... | collective-permute-start | bytes 196616 | tf_op jit(solution)/shard_map/ppermute | solution.py:21
  12.8 84.9 %collective-permute-start.4 = (f32[8,2048]{1,0:T(8,128)S(1)}, f32[8,2048]{1,0:T(8,128)S(1)}, u32[]{:S(2)}, u32[]{:S(2)}) collective-permute-start(f32[8,2048]{1,0:T(8,128)S(1)} %get-tuple-element.18), channel_id=1, source_target_pairs={{0,160},{32,128},{64,224},{96,192},{128,32},{160,0},{192,96},{224,... | collective-permute-start | bytes 196616 | tf_op jit(solution)/shard_map/ppermute | solution.py:21
  12.8 87.4 %all-to-all-start = ((f32[8,8,2048]{2,0,1:T(8,128)}), f32[8,8,2048]{2,0,1:T(8,128)S(1)}, u32[]{:S(2)}, u32[]{:S(2)}) async-start(f32[8,8,2048]{2,0,1:T(8,128)} %bitcast), calls=%async_computation | async-start | bytes 1048576 | tf_op jit(solution)/shard_map/all_to_all | solution.py:68
  19.1 1.0 copy-start.2
  20.2 0.7 copy-start.3
  21.0 0.7 copy-start.4
  92.7 7.4 %collective-permute-start.5 = (f32[8,2048]{1,0:T(8,128)S(1)}, f32[8,2048]{1,0:T(8,128)S(1)}, u32[]{:S(2)}, u32[]{:S(2)}) collective-permute-start(f32[8,2048]{1,0:T(8,128)S(1)} %get-tuple-element.24), channel_id=1, source_target_pairs={{0,192},{32,224},{64,128},{96,160},{128,64},{160,96},{192,0},{224,... | collective-permute-start | bytes 196616 | tf_op jit(solution)/shard_map/ppermute | solution.py:21
  96.9 9.6 %collective-permute-start.6 = (f32[8,2048]{1,0:T(8,128)S(1)}, f32[8,2048]{1,0:T(8,128)S(1)}, u32[]{:S(2)}, u32[]{:S(2)}) collective-permute-start(f32[8,2048]{1,0:T(8,128)S(1)} %get-tuple-element.17), channel_id=1, source_target_pairs={{0,224},{32,192},{64,160},{96,128},{128,96},{160,64},{192,32},{224... | collective-permute-start | bytes 196616 | tf_op jit(solution)/shard_map/ppermute | solution.py:21
  100.2 84.1 %all-to-all-start.1 = ((f32[8,8,2048]{2,0,1:T(8,128)}), f32[8,8,2048]{2,0,1:T(8,128)S(1)}, u32[]{:S(2)}, u32[]{:S(2)}) async-start(f32[8,8,2048]{2,0,1:T(8,128)} %bitcast.13), calls=%async_computation.1 | async-start | bytes 1048576 | tf_op jit(solution)/shard_map/all_to_all | solution.py:74
  208.2 12.9 %collective-permute-start.7 = (f32[8,2048]{1,0:T(8,128)S(1)}, f32[8,2048]{1,0:T(8,128)S(1)}, u32[]{:S(2)}, u32[]{:S(2)}) collective-permute-start(f32[8,2048]{1,0:T(8,128)S(1)} %get-tuple-element.15), channel_id=1, source_target_pairs={{0,32},{32,0},{64,96},{96,64},{128,160},{160,128},{192,224},{224,1... | collective-permute-start | bytes 196616 | tf_op jit(solution)/shard_map/ppermute | solution.py:21
  208.9 106.4 %all-to-all-start.3 = ((f32[8,8,2048]{2,0,1:T(8,128)}), f32[8,8,2048]{2,0,1:T(8,128)S(1)}, u32[]{:S(2)}, u32[]{:S(2)}) async-start(f32[8,8,2048]{2,0,1:T(8,128)} %bitcast.21), calls=%async_computation.3 | async-start | bytes 1048576 | tf_op jit(solution)/shard_map/all_to_all | solution.py:74
  212.4 22.2 %collective-permute-start.8 = (f32[8,2048]{1,0:T(8,128)S(1)}, f32[8,2048]{1,0:T(8,128)S(1)}, u32[]{:S(2)}, u32[]{:S(2)}) collective-permute-start(f32[8,2048]{1,0:T(8,128)S(1)} %get-tuple-element.14), channel_id=1, source_target_pairs={{0,64},{32,96},{64,0},{96,32},{128,192},{160,224},{192,128},{224,1... | collective-permute-start | bytes 196616 | tf_op jit(solution)/shard_map/ppermute | solution.py:21
  215.2 21.3 %collective-permute-start.9 = (f32[8,2048]{1,0:T(8,128)S(1)}, f32[8,2048]{1,0:T(8,128)S(1)}, u32[]{:S(2)}, u32[]{:S(2)}) collective-permute-start(f32[8,2048]{1,0:T(8,128)S(1)} %get-tuple-element.13), channel_id=1, source_target_pairs={{0,96},{32,64},{64,32},{96,0},{128,224},{160,192},{192,160},{224,1... | collective-permute-start | bytes 196616 | tf_op jit(solution)/shard_map/ppermute | solution.py:21
  216.7 20.2 %collective-permute-start.10 = (f32[8,2048]{1,0:T(8,128)S(1)}, f32[8,2048]{1,0:T(8,128)S(1)}, u32[]{:S(2)}, u32[]{:S(2)}) collective-permute-start(f32[8,2048]{1,0:T(8,128)S(1)} %get-tuple-element.12), channel_id=1, source_target_pairs={{0,128},{32,160},{64,192},{96,224},{128,0},{160,32},{192,64},{224,... | collective-permute-start | bytes 196616 | tf_op jit(solution)/shard_map/ppermute | solution.py:21
  221.2 16.9 %collective-permute-start.11 = (f32[8,2048]{1,0:T(8,128)S(1)}, f32[8,2048]{1,0:T(8,128)S(1)}, u32[]{:S(2)}, u32[]{:S(2)}) collective-permute-start(f32[8,2048]{1,0:T(8,128)S(1)} %get-tuple-element.11), channel_id=1, source_target_pairs={{0,160},{32,128},{64,224},{96,192},{128,32},{160,0},{192,96},{224,... | collective-permute-start | bytes 196616 | tf_op jit(solution)/shard_map/ppermute | solution.py:21
  221.2 16.9 %collective-permute-start.12 = (f32[8,2048]{1,0:T(8,128)S(1)}, f32[8,2048]{1,0:T(8,128)S(1)}, u32[]{:S(2)}, u32[]{:S(2)}) collective-permute-start(f32[8,2048]{1,0:T(8,128)S(1)} %get-tuple-element.10), channel_id=1, source_target_pairs={{0,192},{32,224},{64,128},{96,160},{128,64},{160,96},{192,0},{224,... | collective-permute-start | bytes 196616 | tf_op jit(solution)/shard_map/ppermute | solution.py:21
  234.6 5.5 %collective-permute-start.13 = (f32[8,2048]{1,0:T(8,128)S(1)}, f32[8,2048]{1,0:T(8,128)S(1)}, u32[]{:S(2)}, u32[]{:S(2)}) collective-permute-start(f32[8,2048]{1,0:T(8,128)S(1)} %get-tuple-element.9), channel_id=1, source_target_pairs={{0,224},{32,192},{64,160},{96,128},{128,96},{160,64},{192,32},{224... | collective-permute-start | bytes 196616 | tf_op jit(solution)/shard_map/ppermute | solution.py:21
